TPU v7x, 32 devices: a whole 2x2x4 slice. The times are simulated.
32 devices in a mesh: group: 4 (over y, core), dom: 8 (over z, x).
Axes of the slice: x: 2, y: 2, z: 4, core: 2. Of those that a mesh axis runs over, the one named last changes fastest.
Arguments:
- features: float32 [4096, 1024], P(('group', 'dom')), may hold values from -6 to 6
- known_mask: int32 [4096], P(('group', 'dom')), may hold values 0 or 1
- local_tile: bfloat16 [4096, 128], P(('group', 'dom')), may hold values from 0 to 1.5, as said below
- peer_tile: bfloat16 [4096, 256], P(('group', 'dom')), may hold values from 0 to 1.5, as said below
- cross_tile: bfloat16 [4096, 128], P(('group', 'dom')), may hold values from 0 to 1.5, as said below
- peer_rows: int32 [4, 8, 8, 32], P('group', 'dom'), may hold values from 0 to 127
- cross_rows: int32 [4, 8, 4, 32], P('group', 'dom'), may hold values from 0 to 127
- labels: int32 [4096], P(('group', 'dom')), may hold values from 0 to 18
- first_weight: bfloat16 [1024, 1024], replicated, may hold values from -0.1875 to 0.1875
- first_bias: float32 [1024], replicated, may hold values from -3 to 3
- second_weight: bfloat16 [1024, 19], replicated, may hold values from -60 to 60
- second_bias: float32 [19], replicated, may hold values from -3 to 3
Outputs:
- imputed: float32 [4096, 1024], P(('group', 'dom'))
- grad_first: float32 [1024, 1024], P('dom')
- grad_first_bias: float32 [1024], replicated
- grad_second: float32 [1024, 19], replicated
- grad_second_bias: float32 [19], replicated
Inputs may be any that keep to these rules, and one draw needn't show every extreme that they name: `local_tile`: each entry is 0 or lies in 0.5 to 1.5; a fraction of about 8 / 128 is nonzero. `peer_tile`: each entry is 0 or lies in 0.5 to 1.5; a fraction of about 6 / 256 is nonzero. `cross_tile`: each entry is 0 or lies in 0.5 to 1.5; a fraction of about 4 / 128 is nonzero.
All inputs are finite; a program needn't handle non-finite values. No bound on the sum of `known_mask` on one device may be relied on, other than what follows from the above.
Results may differ from a plain program's by a relative error of at most 0.0041.
Values sent between devices are 32-bit elements; how exact they have to be, the bound alone decides.
A program may use at most 64 MiB of HBM per device.

v0:
```python
import math
import jax
import jax.numpy as jnp
from jax import lax
from jax.sharding import PartitionSpec as P

SWEEPS = 3


def fetch_halos(current, peer_list, cross_list):
    width = current.shape[1]
    outgoing = current[peer_list.reshape(-1)].reshape(peer_list.shape[2], peer_list.shape[3], width)
    incoming = lax.all_to_all(outgoing, "dom", split_axis=0, concat_axis=0, tiled=True)
    leaving = current[cross_list.reshape(-1)].reshape(
        cross_list.shape[2], cross_list.shape[3], width
    )
    arriving = lax.all_to_all(leaving, "group", split_axis=0, concat_axis=0, tiled=True)
    return (incoming.reshape(-1, width), arriving.reshape(-1, width))


def local(
    features,
    known_mask,
    local_tile,
    peer_tile,
    cross_tile,
    peer_rows,
    cross_rows,
    labels,
    first_weight,
    first_bias,
    second_weight,
    second_bias,
):
    highest = lax.Precision.HIGHEST
    keep = (known_mask == 1)[:, None]
    current = jnp.where(keep, features, jnp.float32(0.0))
    local_full = local_tile.astype(jnp.float32)
    peer_full = peer_tile.astype(jnp.float32)
    cross_full = cross_tile.astype(jnp.float32)
    degree = (
        1.0 + jnp.sum(local_full, axis=1) + jnp.sum(peer_full, axis=1) + jnp.sum(cross_full, axis=1)
    )
    degree = degree[:, None]
    for sweep in range(SWEEPS):
        incoming, arriving = fetch_halos(current, peer_rows, cross_rows)
        summed = current + jnp.dot(
            local_full, current, precision=highest, preferred_element_type=jnp.float32
        )
        summed = summed + jnp.dot(
            peer_full, incoming, precision=highest, preferred_element_type=jnp.float32
        )
        summed = summed + jnp.dot(
            cross_full, arriving, precision=highest, preferred_element_type=jnp.float32
        )
        current = jnp.where(keep, features, summed / degree)
    inputs = current.astype(jnp.bfloat16)
    pre = jnp.dot(inputs, first_weight, preferred_element_type=jnp.float32) + first_bias
    sigma = jax.nn.sigmoid(pre)
    active = (pre * sigma).astype(jnp.bfloat16)
    logits = jnp.dot(active, second_weight, preferred_element_type=jnp.float32) + second_bias
    shifted = logits - jnp.max(logits, axis=1, keepdims=True)
    expo = jnp.exp(shifted)
    probs = expo / jnp.sum(expo, axis=1, keepdims=True)
    classes = second_weight.shape[1]
    onehot = (labels[:, None] == jnp.arange(classes, dtype=jnp.int32)[None, :]).astype(jnp.float32)
    total_nodes = features.shape[0] * lax.axis_size("group") * lax.axis_size("dom")
    dlogits = (probs - onehot) / jnp.float32(math.sqrt(total_nodes))
    dlogits_b = dlogits.astype(jnp.bfloat16)
    second_bias_term = jnp.sum(dlogits, axis=0)
    second_term = lax.dot_general(
        active, dlogits_b, (((0,), (0,)), ((), ())), preferred_element_type=jnp.float32
    )
    back = lax.dot_general(
        dlogits_b, second_weight, (((1,), (1,)), ((), ())), preferred_element_type=jnp.float32
    )
    dpre = (back * sigma * (1.0 + pre * (1.0 - sigma))).astype(jnp.bfloat16)
    first_bias_term = jnp.sum(dpre.astype(jnp.float32), axis=0)
    share = lax.psum_scatter(
        lax.dot_general(inputs, dpre, (((0,), (0,)), ((), ())), preferred_element_type=jnp.float32),
        "dom",
        scatter_dimension=0,
        tiled=True,
    )
    grad_first = lax.psum(share, "group")
    grad_first_bias, grad_second, grad_second_bias = lax.psum(
        (first_bias_term, second_term, second_bias_term), ("group", "dom")
    )
    return (current, grad_first, grad_first_bias, grad_second, grad_second_bias)


def solution(mesh):
    in_specs = (
        P(("group", "dom"), None),
        P(("group", "dom")),
        P(("group", "dom"), None),
        P(("group", "dom"), None),
        P(("group", "dom"), None),
        P("group", "dom", None, None),
        P("group", "dom", None, None),
        P(("group", "dom")),
        P(),
        P(),
        P(),
        P(),
    )
    out_specs = (P(("group", "dom"), None), P("dom", None), P(), P(), P())
    return jax.shard_map(local, mesh=mesh, in_specs=in_specs, out_specs=out_specs, check_vma=False)
```

profile of v0, /device:TPU:0, one launch (start us, length us, event | category | flops | bytes accessed | tf_op | source)
XLA Modules:
  0.0 363.8 jit_solution(1645723564046518858)
XLA Ops:
  12.3 1.6 gather_fusion.1
  13.9 4.3 %all-to-all-start.1 = ((f32[4,32,1024]{2,1,0:T(8,128)}), f32[4,32,1024]{2,1,0:T(8,128)}, u32[]{:S(2)}, u32[]{:S(2)}) async-start(f32[4,32,1024]{2,1,0:T(8,128)} %bitcast.91), calls=%async_computation.1 | async-start | bytes 1048576 | tf_op jit(solution)/shard_map/all_to_all | solution.py:17
  18.2 2.1 gather_fusion
  20.3 7.3 %all-to-all-done.1 = f32[4,32,1024]{2,1,0:T(8,128)} async-done(((f32[4,32,1024]{2,1,0:T(8,128)}), f32[4,32,1024]{2,1,0:T(8,128)}, u32[]{:S(2)}, u32[]{:S(2)}) %all-to-all-start.1) | async-done | bytes 524320 | tf_op jit(solution)/shard_map/all_to_all | solution.py:17
  27.6 6.6 %all-to-all-start = ((f32[8,32,1024]{2,1,0:T(8,128)}), f32[8,32,1024]{2,1,0:T(8,128)}, u32[]{:S(2)}, u32[]{:S(2)}) async-start(f32[8,32,1024]{2,1,0:T(8,128)} %bitcast.88), calls=%async_computation | async-start | bytes 2097152 | tf_op jit(solution)/shard_map/all_to_all | solution.py:13
  34.4 1.6 convolution_bitcast_fusion.4
  36.1 23.8 %all-to-all-done = f32[8,32,1024]{2,1,0:T(8,128)} async-done(((f32[8,32,1024]{2,1,0:T(8,128)}), f32[8,32,1024]{2,1,0:T(8,128)}, u32[]{:S(2)}, u32[]{:S(2)}) %all-to-all-start) | async-done | bytes 1048608 | tf_op jit(solution)/shard_map/all_to_all | solution.py:13
  59.9 2.2 convolution_bitcast_fusion.8
  64.6 1.6 gather_fusion.3
  66.1 4.1 %all-to-all-start.3 = ((f32[4,32,1024]{2,1,0:T(8,128)}), f32[4,32,1024]{2,1,0:T(8,128)}, u32[]{:S(2)}, u32[]{:S(2)}) async-start(f32[4,32,1024]{2,1,0:T(8,128)} %bitcast.93), calls=%async_computation.3 | async-start | bytes 1048576 | tf_op jit(solution)/shard_map/all_to_all | solution.py:17
  70.3 2.1 gather_fusion.2
  72.4 6.8 %all-to-all-done.3 = f32[4,32,1024]{2,1,0:T(8,128)} async-done(((f32[4,32,1024]{2,1,0:T(8,128)}), f32[4,32,1024]{2,1,0:T(8,128)}, u32[]{:S(2)}, u32[]{:S(2)}) %all-to-all-start.3) | async-done | bytes 524320 | tf_op jit(solution)/shard_map/all_to_all | solution.py:17
  79.2 4.4 %all-to-all-start.2 = ((f32[8,32,1024]{2,1,0:T(8,128)}), f32[8,32,1024]{2,1,0:T(8,128)}, u32[]{:S(2)}, u32[]{:S(2)}) async-start(f32[8,32,1024]{2,1,0:T(8,128)} %bitcast.90), calls=%async_computation.2 | async-start | bytes 2097152 | tf_op jit(solution)/shard_map/all_to_all | solution.py:13
  83.6 2.4 convolution_bitcast_fusion.2
  86.0 23.3 %all-to-all-done.2 = f32[8,32,1024]{2,1,0:T(8,128)} async-done(((f32[8,32,1024]{2,1,0:T(8,128)}), f32[8,32,1024]{2,1,0:T(8,128)}, u32[]{:S(2)}, u32[]{:S(2)}) %all-to-all-start.2) | async-done | bytes 1048608 | tf_op jit(solution)/shard_map/all_to_all | solution.py:13
  109.3 2.2 convolution_bitcast_fusion.7
  111.6 2.2 fusion.11
  115.0 1.6 gather_fusion.5
  116.6 4.1 %all-to-all-start.5 = ((f32[4,32,1024]{2,1,0:T(8,128)}), f32[4,32,1024]{2,1,0:T(8,128)}, u32[]{:S(2)}, u32[]{:S(2)}) async-start(f32[4,32,1024]{2,1,0:T(8,128)} %bitcast.92), calls=%async_computation.5 | async-start | bytes 1048576 | tf_op jit(solution)/shard_map/all_to_all | solution.py:17
  120.8 2.1 gather_fusion.4
  122.8 6.8 %all-to-all-done.5 = f32[4,32,1024]{2,1,0:T(8,128)} async-done(((f32[4,32,1024]{2,1,0:T(8,128)}), f32[4,32,1024]{2,1,0:T(8,128)}, u32[]{:S(2)}, u32[]{:S(2)}) %all-to-all-start.5) | async-done | bytes 524320 | tf_op jit(solution)/shard_map/all_to_all | solution.py:17
  129.6 4.2 %all-to-all-start.4 = ((f32[8,32,1024]{2,1,0:T(8,128)}), f32[8,32,1024]{2,1,0:T(8,128)}, u32[]{:S(2)}, u32[]{:S(2)}) async-start(f32[8,32,1024]{2,1,0:T(8,128)} %bitcast.89), calls=%async_computation.4 | async-start | bytes 2097152 | tf_op jit(solution)/shard_map/all_to_all | solution.py:13
  133.9 2.4 convolution_bitcast_fusion
  136.4 23.3 %all-to-all-done.4 = f32[8,32,1024]{2,1,0:T(8,128)} async-done(((f32[8,32,1024]{2,1,0:T(8,128)}), f32[8,32,1024]{2,1,0:T(8,128)}, u32[]{:S(2)}, u32[]{:S(2)}) %all-to-all-start.4) | async-done | bytes 1048608 | tf_op jit(solution)/shard_map/all_to_all | solution.py:13
  159.6 2.2 convolution_bitcast_fusion.6
  161.9 1.8 fusion.15
  165.2 2.6 fusion.17
  168.8 86.5 %reduce-scatter.2.cloned.1.call-done = f32[128,1024]{1,0:T(8,128)} async-done(((f32[1024,1024]{1,0:T(8,128)}), f32[128,1024]{1,0:T(8,128)}) %reduce-scatter.2.cloned.1.call-update) | async-done | bytes 524304 | tf_op jit(solution)/shard_map/reduce_scatter | solution.py:79
  256.5 40.4 %all-reduce = (f32[1024]{0:T(1024)}, f32[19]{0:T(128)}) all-reduce(f32[1024]{0:T(1024)S(1)} %get-tuple-element.16, f32[19]{0:T(128)S(1)} %fusion.26), channel_id=1, replica_groups=mesh['group'=4,'dom'=8] {'group','dom'}, use_global_device_ids=true, to_apply=%region_8.9 | all-reduce | flops 1043 | bytes 8344 | tf_op jit(solution)/shard_map/psum | solution.py:86
  296.8 19.7 %all-reduce.6.cloned.1.call-done = f32[1024,19]{0,1:T(8,128)} async-done(((f32[1024,19]{0,1:T(8,128)}), f32[1024,19]{0,1:T(8,128)}) %all-reduce.6.cloned.1.call-update) | async-done | bytes 77840 | tf_op jit(solution)/shard_map/psum | solution.py:86
  316.6 36.4 %all-reduce.4.cloned.1.call-done = f32[128,1024]{1,0:T(8,128)} async-done(((f32[128,1024]{1,0:T(8,128)}), f32[128,1024]{1,0:T(8,128)}) %all-reduce.4.cloned.1.call-update) | async-done | bytes 524304 | tf_op jit(solution)/shard_map/psum | solution.py:85
  353.0 1.9 copy.30
  (52 shorter events, 13.2 us)
Async XLA Ops:
  8.0 155.8 %copy-start = (bf16[1024,1024]{1,0:T(8,128)(2,1)S(1)}, bf16[1024,1024]{1,0:T(8,128)(2,1)}, u32[]{:S(2)}) copy-start(bf16[1024,1024]{1,0:T(8,128)(2,1)} %param.20) | copy-start | bytes 6291460
  8.0 4.1 %copy-start.7 = (s32[1,1,4,32]{3,2,1,0:T(4,128)S(1)}, s32[1,1,4,32]{3,2,1,0:T(4,128)}, u32[]{:S(2)}) copy-start(s32[1,1,4,32]{3,2,1,0:T(4,128)} %param.18) | copy-start | bytes 1540
  12.3 5.9 %copy-start.5 = (s32[1,1,8,32]{3,2,1,0:T(8,128)S(1)}, s32[1,1,8,32]{3,2,1,0:T(8,128)}, u32[]{:S(2)}) copy-start(s32[1,1,8,32]{3,2,1,0:T(8,128)} %param.17) | copy-start | bytes 3076
  13.9 13.7 %all-to-all-start.1 = ((f32[4,32,1024]{2,1,0:T(8,128)}), f32[4,32,1024]{2,1,0:T(8,128)}, u32[]{:S(2)}, u32[]{:S(2)}) async-start(f32[4,32,1024]{2,1,0:T(8,128)} %bitcast.91), calls=%async_computation.1 | async-start | bytes 1048576 | tf_op jit(solution)/shard_map/all_to_all | solution.py:17
  20.3 13.9 %copy-start.2 = (bf16[128,256]{1,0:T(8,128)(2,1)S(1)}, bf16[128,256]{1,0:T(8,128)(2,1)}, u32[]{:S(2)}) copy-start(bf16[128,256]{1,0:T(8,128)(2,1)} %param.15) | copy-start | bytes 196612
  20.3 14.0 %copy-start.3 = (bf16[128,128]{1,0:T(8,128)(2,1)S(1)}, bf16[128,128]{1,0:T(8,128)(2,1)}, u32[]{:S(2)}) copy-start(bf16[128,128]{1,0:T(8,128)(2,1)} %param.16) | copy-start | bytes 98308
  20.3 14.0 %copy-start.4 = (bf16[128,128]{1,0:T(8,128)(2,1)S(1)}, bf16[128,128]{1,0:T(8,128)(2,1)}, u32[]{:S(2)}) copy-start(bf16[128,128]{1,0:T(8,128)(2,1)} %param.14) | copy-start | bytes 98308
  27.6 32.3 %all-to-all-start = ((f32[8,32,1024]{2,1,0:T(8,128)}), f32[8,32,1024]{2,1,0:T(8,128)}, u32[]{:S(2)}, u32[]{:S(2)}) async-start(f32[8,32,1024]{2,1,0:T(8,128)} %bitcast.88), calls=%async_computation | async-start | bytes 2097152 | tf_op jit(solution)/shard_map/all_to_all | solution.py:13
  66.1 13.0 %all-to-all-start.3 = ((f32[4,32,1024]{2,1,0:T(8,128)}), f32[4,32,1024]{2,1,0:T(8,128)}, u32[]{:S(2)}, u32[]{:S(2)}) async-start(f32[4,32,1024]{2,1,0:T(8,128)} %bitcast.93), calls=%async_computation.3 | async-start | bytes 1048576 | tf_op jit(solution)/shard_map/all_to_all | solution.py:17
  79.2 32.4 %copy-start.1 = (f32[128,1024]{0,1:T(8,128)S(1)}, f32[128,1024]{0,1:T(8,128)}, u32[]{:S(2)}) copy-start(f32[128,1024]{0,1:T(8,128)} %fusion.7) | copy-start | bytes 1572868
  79.2 30.1 %all-to-all-start.2 = ((f32[8,32,1024]{2,1,0:T(8,128)}), f32[8,32,1024]{2,1,0:T(8,128)}, u32[]{:S(2)}, u32[]{:S(2)}) async-start(f32[8,32,1024]{2,1,0:T(8,128)} %bitcast.90), calls=%async_computation.2 | async-start | bytes 2097152 | tf_op jit(solution)/shard_map/all_to_all | solution.py:13
  116.6 13.0 %all-to-all-start.5 = ((f32[4,32,1024]{2,1,0:T(8,128)}), f32[4,32,1024]{2,1,0:T(8,128)}, u32[]{:S(2)}, u32[]{:S(2)}) async-start(f32[4,32,1024]{2,1,0:T(8,128)} %bitcast.92), calls=%async_computation.5 | async-start | bytes 1048576 | tf_op jit(solution)/shard_map/all_to_all | solution.py:17
  129.6 30.0 %all-to-all-start.4 = ((f32[8,32,1024]{2,1,0:T(8,128)}), f32[8,32,1024]{2,1,0:T(8,128)}, u32[]{:S(2)}, u32[]{:S(2)}) async-start(f32[8,32,1024]{2,1,0:T(8,128)} %bitcast.89), calls=%async_computation.4 | async-start | bytes 2097152 | tf_op jit(solution)/shard_map/all_to_all | solution.py:13
  133.9 121.4 %reduce-scatter.2.cloned.1.call-start = ((), (), s32[]{:S(2)}) async-start(), calls=%async_computation.7 | async-start | bytes 4718592 | tf_op jit(solution)/shard_map/reduce_scatter | solution.py:79
  159.6 4.1 %copy-start.9 = (f32[1024]{0:T(1024)S(1)}, f32[1024]{0:T(1024)}, u32[]{:S(2)}) copy-start(f32[1024]{0:T(1024)} %param.21) | copy-start | bytes 12292
  163.8 0.8 copy-start.8
  163.8 0.8 copy-start.10
  163.8 1.0 copy-start.6
  167.8 148.7 %all-reduce.6.cloned.1.call-start = ((), (), s32[]{:S(2)}) async-start(), calls=%async_computation.9 | async-start | bytes 196608 | tf_op jit(solution)/shard_map/psum | solution.py:86
  168.7 184.3 %all-reduce.4.cloned.1.call-start = ((), (), s32[]{:S(2)}) async-start(), calls=%async_computation.8 | async-start | bytes 1048576 | tf_op jit(solution)/shard_map/psum | solution.py:85
Sparse Core Ops, SparseCore 0:
  168.0 87.3 reduce-scatter.1
Sparse Core Ops, SparseCore 1:
  174.5 142.0 all-reduce.5
  318.8 34.2 all-reduce.3
where the time goes:
time: 365 us; the launch traced here: 364 us
  waiting for transfers between devices  234 us (64%)
  blocking collectives  40.4 us (11%)
  starting transfers between devices  27.9 us (8%)
  matrix products  23 us (6%)
  local copies, waits for them, and re-layouts  20.8 us (6%)
  between operations  15.7 us (4%)
    reduce_scatter x1, waiting for transfers between devices, local(): lax.psum_scatter(lax.dot_general(inputs, dpre, (((0,), (0,)), ((), ())),...  86.5 us
    all_to_all x3, waiting for transfers between devices, fetch_halos(): lax.all_to_all(outgoing, 'dom', split_axis=0, concat_axis=0, tiled=True)  70.4 us
    psum x1, blocking collectives, local(): lax.psum((first_bias_term, second_term, second_bias_term), ('group', 'dom'))  40.4 us
    psum x1, waiting for transfers between devices, local(): grad_first = lax.psum(share, 'group')  36.4 us
    all_to_all x3, waiting for transfers between devices, fetch_halos(): lax.all_to_all(leaving, 'group', split_axis=0, concat_axis=0, tiled=True)  20.9 us
    psum x1, waiting for transfers between devices, local(): lax.psum((first_bias_term, second_term, second_bias_term), ('group', 'dom'))  19.7 us
    all_to_all x3, starting transfers between devices, fetch_halos(): lax.all_to_all(outgoing, 'dom', split_axis=0, concat_axis=0, tiled=True)  15.2 us
    all_to_all x3, starting transfers between devices, fetch_halos(): lax.all_to_all(leaving, 'group', split_axis=0, concat_axis=0, tiled=True)  12.6 us
  transfers between devices with their start and end apart: 9, of which 9 were waited for; matrix products, arithmetic and copies ran while one was open for 4% of the time, Pallas kernels for 0%

commit v1 on v0

--- a/solution.py
+++ b/solution.py
@@ -82,7 +82,7 @@
         scatter_dimension=0,
         tiled=True,
     )
-    grad_first = lax.psum(share, "group")
+    grad_first = jnp.sum(lax.all_gather(share, "group"), axis=0)
     grad_first_bias, grad_second, grad_second_bias = lax.psum(
         (first_bias_term, second_term, second_bias_term), ("group", "dom")
     )

time: 365 us -> 402 us (1.10)
  waiting for transfers between devices: 234 us -> 270 us
    psum x1, waiting for transfers between devices: 19.7 us -> 91.7 us  [local(): lax.psum((first_bias_term, second_term, second_bias_term), ('group', 'dom'))]
    psum x1 -> x0, waiting for transfers between devices: 36.4 us -> none  [local(): grad_first = lax.psum(share, 'group')]
  transfers between devices with their start and end apart: 9 -> 9, of which waited for: 9 -> 8; matrix products, arithmetic and copies ran while one was open for 4% -> 4% of each run, Pallas kernels for 0% -> 0%
where the time goes in v1:
time: 402 us; the launch traced here: 401 us
  waiting for transfers between devices  270 us (67%)
  blocking collectives  40.6 us (10%)
  starting transfers between devices  27.9 us (7%)
  matrix products  23 us (6%)
  local copies, waits for them, and re-layouts  19 us (5%)
  between operations  15.7 us (4%)
  other arithmetic  4.49 us (1%)
    psum x1, waiting for transfers between devices, local(): lax.psum((first_bias_term, second_term, second_bias_term), ('group', 'dom'))  91.7 us
    reduce_scatter x1, waiting for transfers between devices, local(): lax.psum_scatter(lax.dot_general(inputs, dpre, (((0,), (0,)), ((), ())),...  86.7 us
    all_to_all x3, waiting for transfers between devices, fetch_halos(): lax.all_to_all(outgoing, 'dom', split_axis=0, concat_axis=0, tiled=True)  70.4 us
    psum x1, blocking collectives, local(): lax.psum((first_bias_term, second_term, second_bias_term), ('group', 'dom'))  40.6 us
    all_to_all x3, waiting for transfers between devices, fetch_halos(): lax.all_to_all(leaving, 'group', split_axis=0, concat_axis=0, tiled=True)  20.9 us
    all_to_all x3, starting transfers between devices, fetch_halos(): lax.all_to_all(outgoing, 'dom', split_axis=0, concat_axis=0, tiled=True)  15.2 us
    all_to_all x3, starting transfers between devices, fetch_halos(): lax.all_to_all(leaving, 'group', split_axis=0, concat_axis=0, tiled=True)  12.6 us
  transfers between devices with their start and end apart: 9, of which 8 were waited for; matrix products, arithmetic and copies ran while one was open for 4% of the time, Pallas kernels for 0%

profile of v1, /device:TPU:0, one launch (start us, length us, event | category | flops | bytes accessed | tf_op | source)
XLA Modules:
  0.0 400.5 jit_solution(8676224123350819510)
XLA Ops:
  12.3 1.6 gather_fusion.1
  13.9 4.3 %all-to-all-start.1 = ((f32[4,32,1024]{2,1,0:T(8,128)}), f32[4,32,1024]{2,1,0:T(8,128)}, u32[]{:S(2)}, u32[]{:S(2)}) async-start(f32[4,32,1024]{2,1,0:T(8,128)} %bitcast.92), calls=%async_computation.1 | async-start | bytes 1048576 | tf_op jit(solution)/shard_map/all_to_all | solution.py:17
  18.2 2.1 gather_fusion
  20.3 7.3 %all-to-all-done.1 = f32[4,32,1024]{2,1,0:T(8,128)} async-done(((f32[4,32,1024]{2,1,0:T(8,128)}), f32[4,32,1024]{2,1,0:T(8,128)}, u32[]{:S(2)}, u32[]{:S(2)}) %all-to-all-start.1) | async-done | bytes 524320 | tf_op jit(solution)/shard_map/all_to_all | solution.py:17
  27.6 6.6 %all-to-all-start = ((f32[8,32,1024]{2,1,0:T(8,128)}), f32[8,32,1024]{2,1,0:T(8,128)}, u32[]{:S(2)}, u32[]{:S(2)}) async-start(f32[8,32,1024]{2,1,0:T(8,128)} %bitcast.89), calls=%async_computation | async-start | bytes 2097152 | tf_op jit(solution)/shard_map/all_to_all | solution.py:13
  34.4 1.6 convolution_bitcast_fusion.4
  36.1 23.8 %all-to-all-done = f32[8,32,1024]{2,1,0:T(8,128)} async-done(((f32[8,32,1024]{2,1,0:T(8,128)}), f32[8,32,1024]{2,1,0:T(8,128)}, u32[]{:S(2)}, u32[]{:S(2)}) %all-to-all-start) | async-done | bytes 1048608 | tf_op jit(solution)/shard_map/all_to_all | solution.py:13
  59.9 2.2 convolution_bitcast_fusion.8
  64.6 1.6 gather_fusion.3
  66.1 4.1 %all-to-all-start.3 = ((f32[4,32,1024]{2,1,0:T(8,128)}), f32[4,32,1024]{2,1,0:T(8,128)}, u32[]{:S(2)}, u32[]{:S(2)}) async-start(f32[4,32,1024]{2,1,0:T(8,128)} %bitcast.94), calls=%async_computation.3 | async-start | bytes 1048576 | tf_op jit(solution)/shard_map/all_to_all | solution.py:17
  70.3 2.1 gather_fusion.2
  72.4 6.8 %all-to-all-done.3 = f32[4,32,1024]{2,1,0:T(8,128)} async-done(((f32[4,32,1024]{2,1,0:T(8,128)}), f32[4,32,1024]{2,1,0:T(8,128)}, u32[]{:S(2)}, u32[]{:S(2)}) %all-to-all-start.3) | async-done | bytes 524320 | tf_op jit(solution)/shard_map/all_to_all | solution.py:17
  79.2 4.4 %all-to-all-start.2 = ((f32[8,32,1024]{2,1,0:T(8,128)}), f32[8,32,1024]{2,1,0:T(8,128)}, u32[]{:S(2)}, u32[]{:S(2)}) async-start(f32[8,32,1024]{2,1,0:T(8,128)} %bitcast.91), calls=%async_computation.2 | async-start | bytes 2097152 | tf_op jit(solution)/shard_map/all_to_all | solution.py:13
  83.6 2.4 convolution_bitcast_fusion.2
  86.0 23.3 %all-to-all-done.2 = f32[8,32,1024]{2,1,0:T(8,128)} async-done(((f32[8,32,1024]{2,1,0:T(8,128)}), f32[8,32,1024]{2,1,0:T(8,128)}, u32[]{:S(2)}, u32[]{:S(2)}) %all-to-all-start.2) | async-done | bytes 1048608 | tf_op jit(solution)/shard_map/all_to_all | solution.py:13
  109.3 2.2 convolution_bitcast_fusion.7
  111.6 2.2 fusion.11
  115.0 1.6 gather_fusion.5
  116.6 4.1 %all-to-all-start.5 = ((f32[4,32,1024]{2,1,0:T(8,128)}), f32[4,32,1024]{2,1,0:T(8,128)}, u32[]{:S(2)}, u32[]{:S(2)}) async-start(f32[4,32,1024]{2,1,0:T(8,128)} %bitcast.93), calls=%async_computation.5 | async-start | bytes 1048576 | tf_op jit(solution)/shard_map/all_to_all | solution.py:17
  120.8 2.1 gather_fusion.4
  122.8 6.8 %all-to-all-done.5 = f32[4,32,1024]{2,1,0:T(8,128)} async-done(((f32[4,32,1024]{2,1,0:T(8,128)}), f32[4,32,1024]{2,1,0:T(8,128)}, u32[]{:S(2)}, u32[]{:S(2)}) %all-to-all-start.5) | async-done | bytes 524320 | tf_op jit(solution)/shard_map/all_to_all | solution.py:17
  129.6 4.2 %all-to-all-start.4 = ((f32[8,32,1024]{2,1,0:T(8,128)}), f32[8,32,1024]{2,1,0:T(8,128)}, u32[]{:S(2)}, u32[]{:S(2)}) async-start(f32[8,32,1024]{2,1,0:T(8,128)} %bitcast.90), calls=%async_computation.4 | async-start | bytes 2097152 | tf_op jit(solution)/shard_map/all_to_all | solution.py:13
  133.9 2.4 convolution_bitcast_fusion
  136.4 23.3 %all-to-all-done.4 = f32[8,32,1024]{2,1,0:T(8,128)} async-done(((f32[8,32,1024]{2,1,0:T(8,128)}), f32[8,32,1024]{2,1,0:T(8,128)}, u32[]{:S(2)}, u32[]{:S(2)}) %all-to-all-start.4) | async-done | bytes 1048608 | tf_op jit(solution)/shard_map/all_to_all | solution.py:13
  159.6 2.2 convolution_bitcast_fusion.6
  161.9 1.8 fusion.15
  165.2 2.6 fusion.17
  167.9 86.7 %reduce-scatter.2.cloned.1.call-done = f32[128,1024]{1,0:T(8,128)} async-done(((f32[1024,1024]{1,0:T(8,128)}), f32[128,1024]{1,0:T(8,128)}) %reduce-scatter.2.cloned.1.call-update) | async-done | bytes 524304 | tf_op jit(solution)/shard_map/reduce_scatter | solution.py:79
  256.6 40.6 %all-reduce = (f32[1024]{0:T(1024)}, f32[19]{0:T(128)}) all-reduce(f32[1024]{0:T(1024)S(1)} %get-tuple-element.16, f32[19]{0:T(128)S(1)} %fusion.26), channel_id=1, replica_groups=mesh['group'=4,'dom'=8] {'group','dom'}, use_global_device_ids=true, to_apply=%region_8.9 | all-reduce | flops 1043 | bytes 8344 | tf_op jit(solution)/shard_map/psum | solution.py:86
  297.2 2.6 reduce_sum.67
  299.9 91.7 %all-reduce.3.cloned.1.call-done = f32[1024,19]{0,1:T(8,128)} async-done(((f32[1024,19]{0,1:T(8,128)}), f32[1024,19]{0,1:T(8,128)}) %all-reduce.3.cloned.1.call-update) | async-done | bytes 77840 | tf_op jit(solution)/shard_map/psum | solution.py:86
  391.6 1.5 copy.29
  (52 shorter events, 11.7 us)
Async XLA Ops:
  8.0 155.8 %copy-start = (bf16[1024,1024]{1,0:T(8,128)(2,1)S(1)}, bf16[1024,1024]{1,0:T(8,128)(2,1)}, u32[]{:S(2)}) copy-start(bf16[1024,1024]{1,0:T(8,128)(2,1)} %param.20) | copy-start | bytes 6291460
  8.0 4.1 %copy-start.7 = (s32[1,1,4,32]{3,2,1,0:T(4,128)S(1)}, s32[1,1,4,32]{3,2,1,0:T(4,128)}, u32[]{:S(2)}) copy-start(s32[1,1,4,32]{3,2,1,0:T(4,128)} %param.18) | copy-start | bytes 1540
  12.3 5.9 %copy-start.5 = (s32[1,1,8,32]{3,2,1,0:T(8,128)S(1)}, s32[1,1,8,32]{3,2,1,0:T(8,128)}, u32[]{:S(2)}) copy-start(s32[1,1,8,32]{3,2,1,0:T(8,128)} %param.17) | copy-start | bytes 3076
  13.9 13.7 %all-to-all-start.1 = ((f32[4,32,1024]{2,1,0:T(8,128)}), f32[4,32,1024]{2,1,0:T(8,128)}, u32[]{:S(2)}, u32[]{:S(2)}) async-start(f32[4,32,1024]{2,1,0:T(8,128)} %bitcast.92), calls=%async_computation.1 | async-start | bytes 1048576 | tf_op jit(solution)/shard_map/all_to_all | solution.py:17
  20.3 13.9 %copy-start.2 = (bf16[128,256]{1,0:T(8,128)(2,1)S(1)}, bf16[128,256]{1,0:T(8,128)(2,1)}, u32[]{:S(2)}) copy-start(bf16[128,256]{1,0:T(8,128)(2,1)} %param.15) | copy-start | bytes 196612
  20.3 14.0 %copy-start.3 = (bf16[128,128]{1,0:T(8,128)(2,1)S(1)}, bf16[128,128]{1,0:T(8,128)(2,1)}, u32[]{:S(2)}) copy-start(bf16[128,128]{1,0:T(8,128)(2,1)} %param.16) | copy-start | bytes 98308
  20.3 14.0 %copy-start.4 = (bf16[128,128]{1,0:T(8,128)(2,1)S(1)}, bf16[128,128]{1,0:T(8,128)(2,1)}, u32[]{:S(2)}) copy-start(bf16[128,128]{1,0:T(8,128)(2,1)} %param.14) | copy-start | bytes 98308
  27.6 32.3 %all-to-all-start = ((f32[8,32,1024]{2,1,0:T(8,128)}), f32[8,32,1024]{2,1,0:T(8,128)}, u32[]{:S(2)}, u32[]{:S(2)}) async-start(f32[8,32,1024]{2,1,0:T(8,128)} %bitcast.89), calls=%async_computation | async-start | bytes 2097152 | tf_op jit(solution)/shard_map/all_to_all | solution.py:13
  66.1 13.0 %all-to-all-start.3 = ((f32[4,32,1024]{2,1,0:T(8,128)}), f32[4,32,1024]{2,1,0:T(8,128)}, u32[]{:S(2)}, u32[]{:S(2)}) async-start(f32[4,32,1024]{2,1,0:T(8,128)} %bitcast.94), calls=%async_computation.3 | async-start | bytes 1048576 | tf_op jit(solution)/shard_map/all_to_all | solution.py:17
  79.2 32.4 %copy-start.1 = (f32[128,1024]{0,1:T(8,128)S(1)}, f32[128,1024]{0,1:T(8,128)}, u32[]{:S(2)}) copy-start(f32[128,1024]{0,1:T(8,128)} %fusion.7) | copy-start | bytes 1572868
  79.2 30.1 %all-to-all-start.2 = ((f32[8,32,1024]{2,1,0:T(8,128)}), f32[8,32,1024]{2,1,0:T(8,128)}, u32[]{:S(2)}, u32[]{:S(2)}) async-start(f32[8,32,1024]{2,1,0:T(8,128)} %bitcast.91), calls=%async_computation.2 | async-start | bytes 2097152 | tf_op jit(solution)/shard_map/all_to_all | solution.py:13
  116.6 13.0 %all-to-all-start.5 = ((f32[4,32,1024]{2,1,0:T(8,128)}), f32[4,32,1024]{2,1,0:T(8,128)}, u32[]{:S(2)}, u32[]{:S(2)}) async-start(f32[4,32,1024]{2,1,0:T(8,128)} %bitcast.93), calls=%async_computation.5 | async-start | bytes 1048576 | tf_op jit(solution)/shard_map/all_to_all | solution.py:17
  129.6 30.0 %all-to-all-start.4 = ((f32[8,32,1024]{2,1,0:T(8,128)}), f32[8,32,1024]{2,1,0:T(8,128)}, u32[]{:S(2)}, u32[]{:S(2)}) async-start(f32[8,32,1024]{2,1,0:T(8,128)} %bitcast.90), calls=%async_computation.4 | async-start | bytes 2097152 | tf_op jit(solution)/shard_map/all_to_all | solution.py:13
  133.9 120.7 %reduce-scatter.2.cloned.1.call-start = ((), (), s32[]{:S(2)}) async-start(), calls=%async_computation.7 | async-start | bytes 4718592 | tf_op jit(solution)/shard_map/reduce_scatter | solution.py:79
  159.6 4.1 %copy-start.9 = (f32[1024]{0:T(1024)S(1)}, f32[1024]{0:T(1024)}, u32[]{:S(2)}) copy-start(f32[1024]{0:T(1024)} %param.21) | copy-start | bytes 12292
  163.8 0.8 copy-start.8
  163.8 0.8 copy-start.10
  163.8 1.0 copy-start.6
  167.8 129.4 %all-gather.3.cloned.1.call-start = ((), (), s32[]{:S(2)}) async-start(), calls=%async_computation.9 | async-start | bytes 2621440 | tf_op jit(solution)/shard_map/all_gather | solution.py:85
  254.6 136.9 %all-reduce.3.cloned.1.call-start = ((), (), s32[]{:S(2)}) async-start(), calls=%async_computation.8 | async-start | bytes 196608 | tf_op jit(solution)/shard_map/psum | solution.py:86
Sparse Core Ops, SparseCore 0:
  168.0 86.5 reduce-scatter.1
  256.1 22.4 all-gather.2
Sparse Core Ops, SparseCore 1:
  261.3 130.2 all-reduce.2
